TPU v7x, 256 devices: a whole 4x4x8 slice. The times are simulated.
256 devices in a mesh: rep: 4 (over z_lo), fsdp: 64 (over x, z_hi, y, core).
Axes of the slice: x: 4, y: 4, z: 8 (z_hi: 2, z_lo: 4; z = z_hi * 4 + z_lo), core: 2. Of those that a mesh axis runs over, the one named last changes fastest.
Arguments:
- latents: bfloat16 [256, 16, 16, 640], P(('rep', 'fsdp')), may hold values from -6 to 6
- cotangent: bfloat16 [256, 16, 16, 640], P(('rep', 'fsdp')), may hold values from -6 to 6
- conv_weight: bfloat16 [4, 5760, 640], P('rep', 'fsdp'), may hold values from -0.078125 to 0.078125
- norm_gain: float32 [4, 640], P('rep'), may hold values from 0.5 to 1.5
- norm_shift: float32 [4, 640], P('rep'), may hold values from -3 to 3
- partner_bit: int32 [64], replicated, may hold values from 0 to 1
Outputs:
- block_out: bfloat16 [256, 16, 16, 640], P(('rep', 'fsdp'))
- input_grad: bfloat16 [256, 16, 16, 640], P(('rep', 'fsdp'))
- weight_grad: float32 [4, 5760, 640], P('rep', 'fsdp')
- norm_grad: float32 [4, 2, 640], P('rep')
Inputs may be any that keep to these rules, and one draw needn't show every extreme that they name: In row shard f, replica r is paired with replica r with bit partner_bit[f] of its index flipped.
All inputs are finite; a program needn't handle non-finite values.
Results may differ from a plain program's by a relative error of at most 0.0065.
Values may be sent and summed in bfloat16 or wider, within the bound.
A program may use at most 128 MiB of HBM per device.

v0:
```python
import jax
import jax.numpy as jnp
from jax import lax
from jax.sharding import PartitionSpec as P

GROUPS = 32


def partner(value, axis, stride):
    mask = 2**stride
    pairs = [(source, source ^ mask) for source in range(lax.axis_size(axis))]
    return lax.ppermute(value, axis, pairs)


def norm_forward(values_in, gain, shift, groups):
    count, side, chans = (values_in.shape[0], values_in.shape[1], values_in.shape[3])
    values = values_in.astype(jnp.float32).reshape(count, side * side, groups, chans // groups)
    center = jnp.mean(values, axis=(1, 3), keepdims=True)
    spread = jnp.mean(jnp.square(values - center), axis=(1, 3), keepdims=True)
    scale_inv = lax.rsqrt(spread + 1e-05)
    normed = (values - center) * scale_inv
    pre_act = normed * gain.reshape(groups, -1) + shift.reshape(groups, -1)
    return (normed, scale_inv, pre_act)


def make_patches(activation):
    count, side, chans = (activation.shape[0], activation.shape[1], activation.shape[3])
    padded = jnp.pad(activation, ((0, 0), (1, 1), (1, 1), (0, 0)))
    pieces = [
        padded[:, row_off : row_off + side, col_off : col_off + side, :]
        for row_off in range(3)
        for col_off in range(3)
    ]
    return jnp.concatenate(pieces, axis=-1).reshape(count * side * side, 9 * chans)


def fold_patches(patch_grad, count, side, chans):
    grads = patch_grad.reshape(count, side, side, 9, chans)
    total = jnp.zeros((count, side + 2, side + 2, chans), jnp.float32)
    for row_off in range(3):
        for col_off in range(3):
            tap = grads[:, :, :, row_off * 3 + col_off, :]
            total = total + jnp.pad(
                tap, ((0, 0), (row_off, 2 - row_off), (col_off, 2 - col_off), (0, 0))
            )
    return total[:, 1:-1, 1:-1, :]


def backward_rest(act_grad, normed, scale_inv, pre_act, gain, groups, inv_batch):
    count, side, chans = (act_grad.shape[0], act_grad.shape[1], act_grad.shape[3])
    act_grad = act_grad.reshape(count, side * side, groups, chans // groups)
    sigma = jax.nn.sigmoid(pre_act)
    pre_grad = act_grad * sigma * (1.0 + pre_act * (1.0 - sigma))
    gain_grad = jnp.sum(pre_grad * normed, axis=(0, 1)).reshape(-1) * inv_batch
    shift_grad = jnp.sum(pre_grad, axis=(0, 1)).reshape(-1) * inv_batch
    normed_grad = pre_grad * gain.reshape(groups, -1)
    first = jnp.mean(normed_grad, axis=(1, 3), keepdims=True)
    second = jnp.mean(normed_grad * normed, axis=(1, 3), keepdims=True)
    input_grad = scale_inv * (normed_grad - first - normed * second)
    return (
        input_grad.reshape(count, side, side, chans).astype(jnp.bfloat16),
        jnp.stack([gain_grad, shift_grad]),
    )


def shards(latents, cotangent, conv_weight, norm_gain, norm_shift, partner_bit):
    count, side, chans = (latents.shape[0], latents.shape[1], latents.shape[3])
    shard_total = lax.axis_size("fsdp")
    inv_batch = 1.0 / (count * shard_total)
    gain = norm_gain[0]
    normed, scale_inv, pre_act = norm_forward(latents, gain, norm_shift[0], GROUPS)
    activation = jax.nn.silu(pre_act).astype(jnp.bfloat16).reshape(count, side, side, chans)
    patches = make_patches(activation)
    cot_rows = cotangent.reshape(count * side * side, chans)
    weight_rows = conv_weight[0]
    output = jnp.dot(
        patches,
        lax.all_gather(weight_rows, "fsdp", axis=0, tiled=True),
        preferred_element_type=jnp.float32,
    )
    patch_grad = lax.dot_general(
        cot_rows,
        lax.all_gather(weight_rows, "fsdp", axis=0, tiled=True),
        (((1,), (1,)), ((), ())),
        preferred_element_type=jnp.float32,
    )
    block_out = output.astype(jnp.bfloat16).reshape(count, side, side, chans)
    act_grad = fold_patches(patch_grad, count, side, chans)
    input_grad, norm_term = backward_rest(
        act_grad, normed, scale_inv, pre_act, gain, GROUPS, inv_batch
    )
    weight_term = (
        lax.dot_general(
            patches, cot_rows, (((0,), (0,)), ((), ())), preferred_element_type=jnp.float32
        )
        * inv_batch
    )
    shard_rows = weight_rows.shape[0]
    term_pieces = weight_term.reshape(shard_total, shard_rows, chans)
    received = lax.all_to_all(
        term_pieces.astype(jnp.bfloat16), "fsdp", split_axis=0, concat_axis=0, tiled=True
    ).astype(term_pieces.dtype)
    weight_shard = jnp.sum(received, axis=0)
    bit_count = lax.axis_size("rep").bit_length() - 1
    shard_bit = lax.dynamic_index_in_dim(partner_bit, lax.axis_index("fsdp"), 0, keepdims=False)
    norm_bit = partner_bit[0]
    norm_total = lax.psum(norm_term, "fsdp")
    weight_avg, norm_avg = (weight_shard, norm_total)
    for bit_index in range(bit_count):
        other_weight, other_norm = (
            partner(weight_shard.astype(jnp.bfloat16), "rep", bit_index).astype(weight_shard.dtype),
            partner(norm_total.astype(jnp.bfloat16), "rep", bit_index).astype(norm_total.dtype),
        )
        weight_avg = jnp.where(
            shard_bit == bit_index, 0.5 * (weight_shard + other_weight), weight_avg
        )
        norm_avg = jnp.where(norm_bit == bit_index, 0.5 * (norm_total + other_norm), norm_avg)
    return (block_out, input_grad, weight_avg[None], norm_avg[None])


def solution(mesh):
    in_specs = (
        P(("rep", "fsdp"), None, None, None),
        P(("rep", "fsdp"), None, None, None),
        P("rep", "fsdp", None),
        P("rep", None),
        P("rep", None),
        P(),
    )
    out_specs = (
        P(("rep", "fsdp"), None, None, None),
        P(("rep", "fsdp"), None, None, None),
        P("rep", "fsdp", None),
        P("rep", None, None),
    )
    return jax.shard_map(shards, mesh=mesh, in_specs=in_specs, out_specs=out_specs, check_vma=False)
```

profile of v0, /device:TPU:0, one launch (start us, length us, event | category | flops | bytes accessed | tf_op | source)
XLA Modules:
  0.0 605.6 jit_solution(758910239517122541)
XLA Ops:
  7.2 1.8 copy.35
  9.1 1.0 convert_reduce_fusion.1
  10.2 0.1 reduce_sum.75
  10.5 1.1 fusion.28
  11.7 0.1 reduce_sum.96
  12.0 0.7 reduce.17
  12.7 0.7 reduce.18
  13.4 144.8 %all-gather.3.cloned.1.call-done = bf16[1,5760,640]{2,0,1:T(2,128)(2,1)} async-done(((bf16[1,90,640]{2,0,1:T(2,128)(2,1)}), bf16[1,5760,640]{2,0,1:T(2,128)(2,1)}) %all-gather.3.cloned.1.call-update) | async-done | bytes 7372816 | tf_op jit(solution)/shard_map/all_gather | solution.py:78
  158.2 9.4 %copy.45 = bf16[1,5760,640]{2,1,0:T(8,128)(2,1)} copy(bf16[1,5760,640]{2,0,1:T(2,128)(2,1)} %all-gather.3.cloned.1.call-done) | data formatting | bytes 14745600
  167.6 5.6 convolution_bitcast_fusion
  173.2 0.4 slice_bitcast_fusion.8
  173.7 0.2 pad_add_fusion
  173.9 0.8 copy-done.2
  174.6 0.9 fusion.27
  176.2 1.1 constant_dynamic-update-slice_fusion.9
  177.3 5.5 fusion
  182.8 9.1 %convert_element_type.71 = bf16[64,90,640]{2,1,0:T(8,128)(2,1)} reshape(bf16[5760,640]{1,0:T(8,128)(2,1)} %fusion) | data formatting | bytes 14745600 | tf_op jit(solution)/shard_map/convert_element_type | solution.py:101
  191.9 6.5 %all-to-all-start = ((bf16[64,90,640]{2,1,0:T(8,128)(2,1)}), bf16[64,90,640]{2,1,0:T(8,128)(2,1)}, u32[]{:S(2)}, u32[]{:S(2)}) async-start(bf16[64,90,640]{2,1,0:T(8,128)(2,1)} %convert_element_type.71), calls=%async_computation | async-start | bytes 15728640 | tf_op jit(solution)/shard_map/all_to_all | solution.py:100
  198.5 0.6 fusion.33
  201.7 354.6 %psum.7 = f32[2,640]{1,0:T(2,128)S(1)} all-reduce(f32[2,640]{1,0:T(2,128)S(1)} %pad_maximum_fusion), channel_id=1, replica_groups=mesh['rep'=4,'fsdp'=64] {'fsdp'}, use_global_device_ids=true, to_apply=%region_11.12 | all-reduce | flops 1280 | bytes 10240 | tf_op jit(solution)/shard_map/psum | solution.py:107
  556.3 9.9 %collective-permute-start.3 = (bf16[2,640]{1,0:T(2,128)(2,1)S(1)}, bf16[2,640]{1,0:T(2,128)(2,1)S(1)}, u32[]{:S(2)}, u32[]{:S(2)}) collective-permute-start(bf16[2,640]{1,0:T(2,128)(2,1)S(1)} %convert_element_type.76), channel_id=1, source_target_pairs={{0,64},{64,0},{128,192},{192,128},{1,65},{65,1},{129,193},{193,129... | collective-permute-start | bytes 7688 | tf_op jit(solution)/shard_map/ppermute | solution.py:12
  566.2 8.0 %collective-permute-start.2 = (bf16[2,640]{1,0:T(2,128)(2,1)S(1)}, bf16[2,640]{1,0:T(2,128)(2,1)S(1)}, u32[]{:S(2)}, u32[]{:S(2)}) collective-permute-start(bf16[2,640]{1,0:T(2,128)(2,1)S(1)} %convert_element_type.76), channel_id=1, source_target_pairs={{0,128},{64,192},{128,0},{192,64},{1,129},{65,193},{129,1},{193,65... | collective-permute-start | bytes 7688 | tf_op jit(solution)/shard_map/ppermute | solution.py:12
  575.0 1.0 constant_dynamic-update-slice_fusion.8
  576.0 1.0 constant_dynamic-update-slice_fusion.7
  577.4 0.9 fusion.26
  578.3 6.4 %fusion.4 = bf16[256,640]{1,0:T(8,128)(2,1)} fusion(bf16[256,5760]{1,0:T(8,128)(2,1)S(1)} %constant_dynamic-update-slice_fusion, bf16[1,5760,640]{2,1,0:T(8,128)(2,1)} %copy.45), kind=kOutput, calls=%fused_computation.7 | convolution fusion | flops 1887600640 | bytes 10649600 | tf_op jit(solution)/shard_map/dot_general | solution.py:76
  584.7 4.5 convert_reduce_fusion
  589.2 1.8 collective-permute-start.1
  591.0 0.6 select_bitcast_fusion
  591.6 2.5 collective-permute-done.1
  594.2 3.7 collective-permute-done
  597.9 0.8 broadcast_in_dim.4
  (55 shorter events, 2.4 us)
Async XLA Ops:
  7.2 160.5 %copy-start = (bf16[1,16,16,640]{3,2,1,0:T(8,128)(2,1)S(1)}, bf16[1,16,16,640]{3,2,1,0:T(8,128)(2,1)}, u32[]{:S(2)}) copy-start(bf16[1,16,16,640]{3,2,1,0:T(8,128)(2,1)} %param.7) | copy-start | bytes 983044
  7.2 151.0 %all-gather.3.cloned.1.call-start = ((), (), s32[]{:S(2)}) async-start(), calls=%async_computation.1 | async-start | bytes 14976000 | tf_op jit(solution)/shard_map/all_gather | solution.py:78
  173.7 1.0 copy-start.2
  191.9 6.5 %copy-start.4 = (s32[64]{0:T(128)S(1)}, s32[64]{0:T(128)}, u32[]{:S(2)}) copy-start(s32[64]{0:T(128)} %param.11) | copy-start | bytes 772
  191.9 385.1 %copy-start.3 = (bf16[1,16,16,640]{3,2,1,0:T(8,128)(2,1)S(1)}, bf16[1,16,16,640]{3,2,1,0:T(8,128)(2,1)}, u32[]{:S(2)}) copy-start(bf16[1,16,16,640]{3,2,1,0:T(8,128)(2,1)} %get-tuple-element.21) | copy-start | bytes 983044
  191.9 392.8 %all-to-all-start = ((bf16[64,90,640]{2,1,0:T(8,128)(2,1)}), bf16[64,90,640]{2,1,0:T(8,128)(2,1)}, u32[]{:S(2)}, u32[]{:S(2)}) async-start(bf16[64,90,640]{2,1,0:T(8,128)(2,1)} %convert_element_type.71), calls=%async_computation | async-start | bytes 15728640 | tf_op jit(solution)/shard_map/all_to_all | solution.py:100
  556.3 34.7 %collective-permute-start.3 = (bf16[2,640]{1,0:T(2,128)(2,1)S(1)}, bf16[2,640]{1,0:T(2,128)(2,1)S(1)}, u32[]{:S(2)}, u32[]{:S(2)}) collective-permute-start(bf16[2,640]{1,0:T(2,128)(2,1)S(1)} %convert_element_type.76), channel_id=1, source_target_pairs={{0,64},{64,0},{128,192},{192,128},{1,65},{65,1},{129,193},{193,129... | collective-permute-start | bytes 7688 | tf_op jit(solution)/shard_map/ppermute | solution.py:12
  566.2 24.9 %collective-permute-start.2 = (bf16[2,640]{1,0:T(2,128)(2,1)S(1)}, bf16[2,640]{1,0:T(2,128)(2,1)S(1)}, u32[]{:S(2)}, u32[]{:S(2)}) collective-permute-start(bf16[2,640]{1,0:T(2,128)(2,1)S(1)} %convert_element_type.76), channel_id=1, source_target_pairs={{0,128},{64,192},{128,0},{192,64},{1,129},{65,193},{129,1},{193,65... | collective-permute-start | bytes 7688 | tf_op jit(solution)/shard_map/ppermute | solution.py:12
  578.3 20.5 %copy-start.1 = (bf16[1,16,16,640]{3,2,1,0:T(8,128)(2,1)S(1)}, bf16[1,16,16,640]{3,2,1,0:T(8,128)(2,1)}, u32[]{:S(2)}) copy-start(bf16[1,16,16,640]{3,2,1,0:T(8,128)(2,1)} %param.7) | copy-start | bytes 983044
  589.2 5.0 collective-permute-start.1
  591.0 6.8 %collective-permute-start = (bf16[90,640]{1,0:T(8,128)(2,1)S(1)}, bf16[90,640]{1,0:T(8,128)(2,1)S(1)}, u32[]{:S(2)}, u32[]{:S(2)}) collective-permute-start(bf16[90,640]{1,0:T(8,128)(2,1)S(1)} %convert_element_type.73), channel_id=1, source_target_pairs={{0,128},{64,192},{128,0},{192,64},{1,129},{65,193},{129,1},{193,65... | collective-permute-start | bytes 345608 | tf_op jit(solution)/shard_map/ppermute | solution.py:12
Sparse Core Ops, SparseCore 0:
  12.1 146.0 all-gather.2
where the time goes:
time: 606 us
  blocking collectives  355 us (59%)
  waiting for transfers between devices  151 us (25%)
  local copies, waits for them, and re-layouts  28.1 us (5%)
  starting transfers between devices  26.3 us (4%)
  matrix products  17.5 us (3%)
  between operations  16.9 us (3%)
  other arithmetic  11.2 us (2%)
    psum x1, blocking collectives, shards(): norm_total = lax.psum(norm_term, 'fsdp')  355 us
    all_gather x1, waiting for transfers between devices, shards(): lax.all_gather(weight_rows, 'fsdp', axis=0, tiled=True)  145 us
    ppermute x4, starting transfers between devices, partner(): return lax.ppermute(value, axis, pairs)  19.7 us
    unnamed x28, local copies, waits for them, and re-layouts  14.9 us
  transfers between devices with their start and end apart: 6, of which 3 were waited for; matrix products, arithmetic and copies ran while one was open for 3% of the time, Pallas kernels for 0%

commit v1 on v0

v1 whole, which is shorter than its diff:
```python
import jax
import jax.numpy as jnp
from jax import lax
from jax.experimental import pallas as pl
from jax.experimental.pallas import tpu as pltpu
from jax.sharding import PartitionSpec as P

GROUPS = 32
SIDE = 16
POS = SIDE * SIDE
SLAB = 96
UNROLL = 4
BF = jnp.bfloat16
F32 = jnp.float32
TAPS = [(a - 1, b - 1) for a in range(3) for b in range(3)]


def order(step):
    return (step + (step // 2) * (1 - 2 * (step % 2)) + 2) % 4


def lane_mask(down, right):
    lane = lax.broadcasted_iota(jnp.int32, (1, POS), 1)
    row, col = lane // SIDE + down, lane % SIDE + right
    return (row >= 0) & (row < SIDE) & (col >= 0) & (col < SIDE)


def kernel(
    lat, cot, w_in, gain, shift, bits, out, in_grad, w_grad, n_grad,
    wg, pt, tall, cs, tm, bacc, xt, nt, at, acc, gcol, scol, rcol, ncol, fin,
    sib_s, sib_r, b2_s, b2_r, b1_s, b1_r, a2_s, a2_r, a1_s, a1_r, z_s, z_r, p_s, p_r,
    n1_s, n1_r, n2_s, n2_r, n3_s, n3_r,
    ag_ss, ag_rs, sib_ss, sib_rs, b2_ss, b2_rs, b1_ss, b1_rs, a2_ss, a2_rs, a1_ss, a1_rs,
    z_ss, z_rs, p_ss, p_rs, n1_ss, n1_rs, n2_ss, n2_rs, n3_ss, n3_rs,
):
    chans = lat.shape[1]
    shard = w_in.shape[0]
    count = wg.shape[0]
    krows = count * shard
    rep, fs = lax.axis_index("rep"), lax.axis_index("fsdp")
    x, z, y, core = fs // 16, (fs // 8) % 2, (fs // 2) % 4, fs % 2
    a, b = x + (y - x) * core, y + (x - y) * core

    def slot(a_, z_, b_, core_):
        return (a_ % 4) * (16 - 14 * core_) + z_ * 8 + (b_ % 4) * (2 + 14 * core_) + core_

    def at_ab(da, db):
        return (rep, slot(a + da, z, b + db, core))

    sibling = (rep, fs + 1 - 2 * core)
    opposite = (rep, slot(a, 1 - z, b, core))
    partners = ((rep + 1 - 2 * (rep % 2), fs), (rep + 2 - 4 * (rep // 2), fs))

    def remote(src, dst, send_sem, recv_sem, device):
        return pltpu.make_async_remote_copy(
            src_ref=src, dst_ref=dst, send_sem=send_sem, recv_sem=recv_sem,
            device_id=device, device_id_type=pl.DeviceIdType.MESH,
        )

    sent = []

    def ag_send(index, *devices):
        for device in devices:
            copy = remote(wg.at[index], wg.at[index], ag_ss.at[len(sent)], ag_rs.at[index], device)
            copy.start()
            sent.append(copy)

    def ag_wait(index):
        remote(wg.at[index], wg.at[index], ag_ss.at[0], ag_rs.at[index], sibling).wait_recv()

    b_both = (at_ab(0, 1), at_ab(0, 3))
    a_both = (at_ab(1, 0), at_ab(3, 0))
    arrivals = [(0, z), (3, z), (1, z), (0, 1 - z), (2, z), (3, 1 - z), (1, 1 - z), (2, 1 - z)]

    def ag_first():
        ag_send(fs, *a_both, opposite, *b_both, sibling)

    def ag_near(zz):
        ag_wait(slot(a + 3, zz, b, core))
        ag_wait(slot(a + 1, zz, b, core))
        ag_send(slot(a + 3 + 2 * zz, zz, b, core), at_ab(1 + 2 * zz, 0))
        ag_send(slot(a + 3, zz, b, core), *b_both, sibling)
        ag_send(slot(a + 1, zz, b, core), *b_both, sibling)

    def ag_opposite():
        own = slot(a, 1 - z, b, core)
        ag_wait(own)
        ag_send(own, *a_both, *b_both, sibling)

    def ag_far(zz):
        own = slot(a + 2, zz, b, core)
        ag_wait(own)
        ag_send(own, *b_both, sibling)

    def ag_b(step):
        da, zz = arrivals[step]
        for db in (3, 1):
            ag_wait(slot(a + da, zz, b + db, core))
        ag_send(slot(a + da, zz, b + 3 + 2 * zz, core), at_ab(0, 1 + 2 * zz))
        for db in (3, 1):
            ag_send(slot(a + da, zz, b + db, core), sibling)

    def ag_b_far(step):
        da, zz = arrivals[step]
        own = slot(a + da, zz, b + 2, core)
        ag_wait(own)
        ag_send(own, sibling)

    def ag_sibling():
        def body(step, carry):
            ag_wait(2 * step + 1 - core)
            return carry

        lax.fori_loop(0, count // 2, body, 0)

    def plane(i):
        return z + (1 - 2 * z) * (1 - i // 4)

    def terms(first, indices):
        lhs = jnp.concatenate([pt[index] for index in indices], axis=0)
        return jnp.dot(lhs, cot[...], preferred_element_type=F32)

    def sib_copy(i):
        return remote(sib_s.at[i], sib_r.at[i], sib_ss.at[i], sib_rs.at[i], sibling)

    def sibling_terms(g):
        todo = [(i, jb) for i in (2 * g, 2 * g + 1) for jb in range(4)]
        value = terms(g, [slot(b + order(i % 4), plane(i), a + order(jb), 1 - core) for i, jb in todo])
        for n, (i, jb) in enumerate(todo):
            sib_s[i, jb] = value[n * SLAB : (n + 1) * SLAB].astype(BF)
            if jb == 3:
                sib_copy(i).start()

    def own_terms(g):
        todo = [(i, jb) for i in (2 * g, 2 * g + 1) for jb in range(4)]
        value = terms(g, [slot(a + order(i % 4), plane(i), b + order(jb), core) for i, jb in todo])
        for n, (i, jb) in enumerate(todo):
            tm[i, jb] = value[n * SLAB : (n + 1) * SLAB]

    def chip_term(i, jb):
        return tm[i, jb] + sib_r[i, jb].astype(F32)

    def b2_copy(i):
        return remote(b2_s.at[i], b2_r.at[i], b2_ss.at[i], b2_rs.at[i], at_ab(0, 1 + 2 * (i % 2)))

    def b1_copy(i, way):
        return remote(
            b1_s.at[i, way], b1_r.at[i, way], b1_ss.at[i, way], b1_rs.at[i, way],
            at_ab(0, 1 + 2 * way),
        )

    def rs_far(i):
        sib_copy(i).wait_recv()
        b2_s[i] = chip_term(i, 0).astype(BF)
        b2_copy(i).start()

    def rs_near(i):
        way = 1 - i % 2
        b1_s[i, way] = chip_term(i, 2 - way).astype(BF)
        b1_copy(i, way).start()

    def rs_late(i):
        way = i % 2
        b2_copy(i).wait_recv()
        b1_s[i, way] = (chip_term(i, 2 - way) + b2_r[i].astype(F32)).astype(BF)
        b1_copy(i, way).start()

    def row_term(i):
        for way in range(2):
            b1_copy(i, way).wait_recv()
        return chip_term(i, 3) + b1_r[i, 0].astype(F32) + b1_r[i, 1].astype(F32)

    def a2_copy(h):
        return remote(a2_s.at[h], a2_r.at[h], a2_ss.at[h], a2_rs.at[h], at_ab(1 + 2 * h, 0))

    def a1_copy(h, way):
        return remote(
            a1_s.at[h, way], a1_r.at[h, way], a1_ss.at[h, way], a1_rs.at[h, way],
            at_ab(1 + 2 * way, 0),
        )

    def rs_a_far(h):
        a2_s[h] = row_term(4 * h).astype(BF)
        a2_copy(h).start()

    def rs_a_near(h):
        way = 1 - h
        a1_s[h, way] = row_term(4 * h + 2 - way).astype(BF)
        a1_copy(h, way).start()

    def rs_a_late(h):
        way = h
        value = row_term(4 * h + 2 - way)
        a2_copy(h).wait_recv()
        a1_s[h, way] = (value + a2_r[h].astype(F32)).astype(BF)
        a1_copy(h, way).start()

    def plane_term(h):
        value = row_term(4 * h + 3)
        for way in range(2):
            a1_copy(h, way).wait_recv()
        return value + a1_r[h, 0].astype(F32) + a1_r[h, 1].astype(F32)

    z_copy = remote(z_s, z_r, z_ss, z_rs, opposite)
    p_copies = [remote(p_s, p_r.at[i], p_ss.at[i], p_rs.at[i], partners[i]) for i in range(2)]

    def rs_other_plane():
        z_s[...] = plane_term(0).astype(BF)
        z_copy.start()

    def rs_own_plane():
        value = plane_term(1)
        z_copy.wait_recv()
        value = value + z_r[...].astype(F32)
        fin[...] = value
        p_s[...] = value.astype(BF)
        for copy in p_copies:
            copy.start()

    def picked(index, first, second):
        second_share = bits[index].astype(F32)
        return first * (1.0 - second_share) + second * second_share

    def rs_partner():
        for copy in p_copies:
            copy.wait_recv()
        other = picked(fs, p_r[0].astype(F32), p_r[1].astype(F32))
        w_grad[...] = ((fin[...] + other) * (0.5 / count))[:shard].reshape(w_grad.shape)

    me1, me2 = x * 2 + core, z * 4 + y

    def peer1(d):
        other = (me1 + d) % 8
        return other, (rep, (other // 2) * 16 + z * 8 + y * 2 + other % 2)

    def peer2(d):
        other = (me2 + d) % 8
        return other, (rep, x * 16 + (other // 4) * 8 + (other % 4) * 2 + core)

    norm_stages = [(n1_s, n1_r, n1_ss, n1_rs, me1, peer1), (n2_s, n2_r, n2_ss, n2_rs, me2, peer2)]

    def norm_copy(stage, d, mine):
        send, recv, send_sems, recv_sems, me, peer = norm_stages[stage]
        other, device = peer(d)
        index = me if mine else other
        return remote(send, recv.at[index], send_sems.at[d], recv_sems.at[index], device)

    def norm_start(stage, value):
        send, recv, _, _, me, _ = norm_stages[stage]
        send[...] = value
        recv[me] = value
        for d in range(1, 8):
            norm_copy(stage, d, True).start()

    def norm_sum(stage):
        for d in range(1, 8):
            norm_copy(stage, d, False).wait_recv()
        recv = norm_stages[stage][1]
        total = recv[0]
        for i in range(1, 8):
            total = total + recv[i]
        return total

    n3_copies = [remote(n3_s, n3_r.at[i], n3_ss.at[i], n3_rs.at[i], partners[i]) for i in range(2)]

    def norm_partner_start():
        n3_s[...] = norm_sum(1)
        for copy in n3_copies:
            copy.start()

    def norm_last():
        for copy in n3_copies:
            copy.wait_recv()
        other = picked(0, n3_r[0], n3_r[1])
        n_grad[...] = ((n3_s[...] + other) * (0.5 / count))[:2]

    block = 40
    half = block // 2
    blocks = chans // block
    width = float(POS * (chans // GROUPS))

    def group_mean(column):
        first = lax.broadcasted_iota(jnp.int32, (block, 1), 0) < half
        low = jnp.sum(jnp.where(first, column, 0.0), axis=0, keepdims=True)
        high = jnp.sum(jnp.where(first, 0.0, column), axis=0, keepdims=True)
        return jnp.where(first, low, high) / width

    def to_columns(row):
        return jnp.broadcast_to(row, (128, chans)).T

    def transposes():
        gcol[...] = to_columns(gain[...])
        scol[...] = to_columns(shift[...])
        for i in range(chans // 128):
            span = slice(i * 128, (i + 1) * 128)
            xt[span, :] = lat[:, span].astype(F32).T

    def norm_forward():
        def body(i, carry):
            for u in range(UNROLL):
                span = pl.ds(pl.multiple_of((i * UNROLL + u) * block, block), block)
                values = xt[span, :]
                centered = values - group_mean(jnp.sum(values, axis=1, keepdims=True))
                spread = group_mean(jnp.sum(centered * centered, axis=1, keepdims=True))
                scale = lax.rsqrt(spread + 1e-5)
                normed = centered * scale
                pre = normed * gcol[span, :1] + scol[span, :1]
                nt[span, :] = normed
                rcol[span, :] = jnp.broadcast_to(scale, (block, 128))
                at[span, :] = pre / (1.0 + jnp.exp(-pre))
            return carry

        lax.fori_loop(0, blocks // UNROLL, body, 0)

    def make_patches():
        tall[krows:, :] = jnp.zeros((8, POS), F32)

        def taps(i, carry):
            start = pl.multiple_of(i * 80, 80)
            values = at[pl.ds(start, 80), :]
            for t, (down, right) in enumerate(TAPS):
                offset = 16 * down + right
                moved = values if offset == 0 else pltpu.roll(values, -offset % POS, 1)
                tall[pl.ds(t * chans + start, 80), :] = jnp.where(lane_mask(down, right), moved, 0.0)
            return carry

        lax.fori_loop(0, chans // 80, taps, 0)
        keep = lax.broadcasted_iota(jnp.int32, (SLAB, 1), 0) < shard

        def slabs(g, carry):
            for j in range(4):
                base, rest = j * shard // 8 * 8, j * shard % 8
                start = pl.multiple_of(g * (4 * shard) + base, 8)
                if rest:
                    values = pltpu.roll(tall[pl.ds(start, SLAB + 8), :], SLAB + 8 - rest, 0)[:SLAB]
                else:
                    values = tall[pl.ds(start, SLAB), :]
                pt[g * 4 + j] = jnp.where(keep, values, 0.0).astype(BF)
            return carry

        lax.fori_loop(0, count // 4, slabs, 0)

    def cotangent_shifts():
        for i in range(chans // 128):
            span = slice(i * 128, (i + 1) * 128)
            at[span, :] = cot[:, span].astype(F32).T

        def taps(i, carry):
            span = pl.ds(pl.multiple_of(i * 80, 80), 80)
            values = at[span, :]
            for t, (down, right) in enumerate(TAPS):
                offset = 16 * down + right
                moved = values if offset == 0 else pltpu.roll(values, offset % POS, 1)
                cs[t, span, :] = jnp.where(lane_mask(-down, -right), moved, 0.0).astype(BF)
            return carry

        lax.fori_loop(0, chans // 80, taps, 0)
        bacc[...] = jnp.zeros_like(bacc)

    def forward(first, last):
        def body(g, carry):
            group = pl.ds(g * 8, 8)
            acc[...] += lax.dot_general(
                pt[group].reshape(8 * SLAB, POS), wg[group].reshape(8 * SLAB, chans),
                (((0,), (0,)), ((), ())), preferred_element_type=F32,
            )
            return carry

        if first == 0:
            acc[...] = jnp.zeros_like(acc)
        lax.fori_loop(first, last, body, 0)
        if last == count // 8:
            out[...] = acc[...].astype(BF)

    def backward_tap(t):
        low = chans * t // shard
        slabs = (chans * t + chans - 1) // shard - low + 1
        grads = jnp.dot(
            wg[low : low + slabs].reshape(slabs * SLAB, chans), cs[t], preferred_element_type=F32
        )
        for j in range(slabs):
            first = shard * (low + j) - chans * t
            rest = first % 8
            start = SLAB + first - rest
            bacc[rest // 2, start : start + SLAB, :] += grads[j * SLAB : (j + 1) * SLAB]

    def backward_rest():
        lane = lax.broadcasted_iota(jnp.int32, (1, 128), 1)

        def one(i):
            start = pl.multiple_of(i * block, block)
            span = pl.ds(start, block)
            act_grad = bacc[0, pl.ds(start + SLAB, block), :]
            for r in (2, 4, 6):
                window = bacc[r // 2, pl.ds(start + SLAB - 8, block + 8), :]
                act_grad += pltpu.roll(window, block + r, 0)[:block]
            normed, gain_col = nt[span, :], gcol[span, :1]
            pre = normed * gain_col + scol[span, :1]
            sigma = 1.0 / (1.0 + jnp.exp(-pre))
            pre_grad = act_grad * sigma * (1.0 + pre * (1.0 - sigma))
            gain_grad = jnp.sum(pre_grad * normed, axis=1, keepdims=True)
            shift_grad = jnp.sum(pre_grad, axis=1, keepdims=True)
            ncol[span, :] = jnp.where(lane == 0, gain_grad, jnp.where(lane == 1, shift_grad, 0.0))
            first = group_mean(shift_grad * gain_col)
            second = group_mean(gain_grad * gain_col)
            xt[span, :] = rcol[span, :1] * (pre_grad * gain_col - first - normed * second)

        def body(i, carry):
            for u in range(UNROLL):
                one(i * UNROLL + u)
            return carry

        lax.fori_loop(0, blocks // UNROLL, body, 0)

    def write_input_grad():
        for i in range(chans // 128):
            span = slice(i * 128, (i + 1) * 128)
            in_grad[:, span] = xt[span, :].T.astype(BF)

    barrier = pltpu.get_barrier_semaphore()
    neighbours = [peer(d)[1] for peer in (peer1, peer2) for d in range(1, 8)] + list(partners)
    for device in neighbours:
        pl.semaphore_signal(barrier, inc=1, device_id=device, device_id_type=pl.DeviceIdType.MESH)
    wg[fs, SLAB - 16 :, :] = jnp.zeros((16, chans), BF)
    wg[fs, :shard, :] = w_in[...]
    transposes()
    pl.semaphore_wait(barrier, len(neighbours))

    ag_first()
    norm_forward()
    ag_near(z)
    make_patches()
    ag_far(z)
    ag_opposite()
    sibling_terms(0)
    own_terms(0)
    sibling_terms(1)
    rs_far(0)
    rs_near(0)
    ag_near(1 - z)
    ag_b(0)
    rs_far(1)
    rs_near(1)
    rs_late(0)
    own_terms(1)
    sibling_terms(2)
    ag_far(1 - z)
    ag_b(1)
    rs_far(2)
    rs_near(2)
    rs_late(1)
    ag_b(2)
    own_terms(2)
    sibling_terms(3)
    rs_far(3)
    rs_near(3)
    rs_late(2)
    rs_a_far(0)
    ag_b(3)
    ag_b_far(0)
    own_terms(3)
    rs_far(4)
    rs_near(4)
    rs_late(3)
    rs_a_near(0)
    ag_b(4)
    ag_b_far(1)
    cotangent_shifts()
    rs_far(5)
    rs_near(5)
    rs_late(4)
    rs_a_late(0)
    ag_b(5)
    ag_b_far(2)
    rs_far(6)
    rs_near(6)
    rs_late(5)
    ag_b(6)
    ag_b_far(3)
    rs_other_plane()
    rs_far(7)
    rs_near(7)
    rs_late(6)
    ag_b(7)
    ag_b_far(4)
    ag_b_far(5)
    rs_late(7)
    rs_a_far(1)
    ag_b_far(6)
    ag_b_far(7)
    rs_a_near(1)
    ag_sibling()
    for t in range(5):
        backward_tap(t)
    rs_a_late(1)
    for t in range(5, 9):
        backward_tap(t)
    rs_own_plane()
    backward_rest()
    norm_start(0, ncol[...].T[:8])
    write_input_grad()
    norm_start(1, norm_sum(0))
    forward(0, 4)
    norm_partner_start()
    forward(4, 8)
    rs_partner()
    norm_last()

    for copy in sent:
        copy.wait_send()
    for i in range(8):
        sib_copy(i).wait_send()
        b2_copy(i).wait_send()
        for way in range(2):
            b1_copy(i, way).wait_send()
    for h in range(2):
        a2_copy(h).wait_send()
        for way in range(2):
            a1_copy(h, way).wait_send()
    z_copy.wait_send()
    for copy in p_copies + n3_copies:
        copy.wait_send()
    for stage in range(2):
        for d in range(1, 8):
            norm_copy(stage, d, True).wait_send()


def shards(latents, cotangent, conv_weight, norm_gain, norm_shift, partner_bit):
    chans = latents.shape[3]
    shard = conv_weight.shape[1]
    count = lax.axis_size("fsdp")
    vmem = pl.BlockSpec(memory_space=pltpu.VMEM)
    piece = (SLAB, chans)
    dma = pltpu.SemaphoreType.DMA
    results = pl.pallas_call(
        kernel,
        out_shape=(
            jax.ShapeDtypeStruct((POS, chans), BF),
            jax.ShapeDtypeStruct((POS, chans), BF),
            jax.ShapeDtypeStruct((shard, 1, chans), F32),
            jax.ShapeDtypeStruct((2, chans), F32),
        ),
        in_specs=[vmem] * 5 + [pl.BlockSpec(memory_space=pltpu.SMEM)],
        out_specs=(vmem,) * 4,
        scratch_shapes=[
            pltpu.VMEM((count, *piece), BF),
            pltpu.VMEM((count, SLAB, POS), BF),
            pltpu.VMEM((count * shard + 8, POS), F32),
            pltpu.VMEM((9, chans, POS), BF),
            pltpu.VMEM((8, 4, *piece), F32),
            pltpu.VMEM((4, chans + 2 * SLAB, POS), F32),
            *[pltpu.VMEM((chans, POS), F32)] * 3,
            pltpu.VMEM((POS, chans), F32),
            *[pltpu.VMEM((chans, 128), F32)] * 4,
            pltpu.VMEM(piece, F32),
            *[pltpu.VMEM((8, 4, *piece), BF)] * 2,
            *[pltpu.VMEM((8, *piece), BF)] * 2,
            *[pltpu.VMEM((8, 2, *piece), BF)] * 2,
            *[pltpu.VMEM((2, *piece), BF)] * 2,
            *[pltpu.VMEM((2, 2, *piece), BF)] * 2,
            *[pltpu.VMEM(piece, BF)] * 2,
            pltpu.VMEM(piece, BF),
            pltpu.VMEM((2, *piece), BF),
            *[pltpu.VMEM((8, chans), F32), pltpu.VMEM((8, 8, chans), F32)] * 2,
            pltpu.VMEM((8, chans), F32),
            pltpu.VMEM((2, 8, chans), F32),
            dma((count,)), dma((count,)),
            dma((8,)), dma((8,)),
            dma((8,)), dma((8,)),
            dma((8, 2)), dma((8, 2)),
            dma((2,)), dma((2,)),
            dma((2, 2)), dma((2, 2)),
            dma, dma,
            dma((2,)), dma((2,)),
            dma((8,)), dma((8,)), dma((8,)), dma((8,)),
            dma((2,)), dma((2,)),
        ],
        compiler_params=pltpu.CompilerParams(
            collective_id=0, has_side_effects=True, vmem_limit_bytes=60 << 20
        ),
        name="block",
    )(
        latents.reshape(POS, chans), cotangent.reshape(POS, chans), conv_weight[0],
        norm_gain, norm_shift, partner_bit,
    )
    block_out, input_grad, weight_grad, norm_grad = results
    return (
        block_out.reshape(latents.shape),
        input_grad.reshape(latents.shape),
        weight_grad.reshape(1, shard, chans),
        norm_grad[None],
    )


def solution(mesh):
    in_specs = (
        P(("rep", "fsdp"), None, None, None),
        P(("rep", "fsdp"), None, None, None),
        P("rep", "fsdp", None),
        P("rep", None),
        P("rep", None),
        P(),
    )
    out_specs = (
        P(("rep", "fsdp"), None, None, None),
        P(("rep", "fsdp"), None, None, None),
        P("rep", "fsdp", None),
        P("rep", None, None),
    )
    return jax.shard_map(shards, mesh=mesh, in_specs=in_specs, out_specs=out_specs, check_vma=False)
```

time: 606 us -> 91.8 us (0.15)
  the two profiles are of different devices: /device:TPU:0 before, /device:TPU:24 now
where the time goes in v1:
time: 91.8 us; the launch traced here: 91.6 us
  Pallas kernels  86.8 us (95%)
  local copies, waits for them, and re-layouts  4.12 us (4%)
    pallas_call x1, Pallas kernels, shards(): pl.pallas_call(kernel, out_shape=(jax.ShapeDtypeStruct((POS, chans), BF),...  86.8 us
    unnamed x10, local copies, waits for them, and re-layouts  4.12 us

profile of v1, /device:TPU:24, one launch (start us, length us, event | category | flops | bytes accessed | tf_op | source)
XLA Modules:
  0.0 91.6 jit_solution(9323708065747152731)
XLA Ops:
  0.6 86.8 %block.1 = (bf16[256,640]{1,0:T(8,128)(2,1)}, bf16[256,640]{1,0:T(8,128)(2,1)}, f32[90,1,640]{2,1,0:T(1,128)}, f32[2,640]{1,0:T(2,128)}) custom-call(bf16[256,640]{1,0:T(8,128)(2,1)} %bitcast.7, bf16[256,640]{1,0:T(8,128)(2,1)} %bitcast.8, bf16[90,640]{1,0:T(8,128)(2,1)} %bitcast.12, f32[1,640]{1,0:T(1,128)} %gain.1, f32[1,640]{1,0:T(1,128)} %shift.1, s32[64]{0:T(128)} %bits.1), custom_call_target="tpu_custom_call" | custom-call | tf_op jit(solution)/shard_map/block/pallas_call | solution.py:535
  87.5 0.0 copy-start
  87.5 1.8 %copy.14 = bf16[1,16,16,640]{3,2,1,0:T(8,128)(2,1)} copy(bf16[1,16,16,640]{3,2,1,0:T(8,128)(2,1)} %bitcast.10) | data formatting | bytes 655360
  89.3 0.0 copy-done
  89.3 0.0 copy-start.1
  89.3 0.7 copy.15
  90.0 0.3 copy-done.1
  90.3 0.0 copy-start.2
  90.3 0.7 copy.16
  91.0 0.0 copy-done.2
  91.0 0.6 copy.17
Async XLA Ops:
  87.5 1.8 %copy-start = (bf16[256,640]{1,0:T(8,128)(2,1)S(1)}, bf16[256,640]{1,0:T(8,128)(2,1)}, u32[]{:S(2)}) copy-start(bf16[256,640]{1,0:T(8,128)(2,1)} %get-tuple-element.9) | copy-start | bytes 983044
  89.3 1.1 %copy-start.1 = (f32[90,1,640]{2,1,0:T(1,128)S(1)}, f32[90,1,640]{2,1,0:T(1,128)}, u32[]{:S(2)}) copy-start(f32[90,1,640]{2,1,0:T(1,128)} %get-tuple-element.10) | copy-start | bytes 691204
  90.3 0.7 copy-start.2

commit v2 on v1

--- a/solution.py
+++ b/solution.py
@@ -70,39 +70,44 @@
 
     b_both = (at_ab(0, 1), at_ab(0, 3))
     a_both = (at_ab(1, 0), at_ab(3, 0))
-    arrivals = [(0, z), (3, z), (1, z), (0, 1 - z), (2, z), (3, 1 - z), (1, 1 - z), (2, 1 - z)]
+    def of_plane(other):
+        return 1 - z if other else z
+
+    arrivals = [(0, 0), (3, 0), (1, 0), (0, 1), (2, 0), (3, 1), (1, 1), (2, 1)]
 
     def ag_first():
-        ag_send(fs, *a_both, opposite, *b_both, sibling)
-
-    def ag_near(zz):
-        ag_wait(slot(a + 3, zz, b, core))
-        ag_wait(slot(a + 1, zz, b, core))
-        ag_send(slot(a + 3 + 2 * zz, zz, b, core), at_ab(1 + 2 * zz, 0))
-        ag_send(slot(a + 3, zz, b, core), *b_both, sibling)
-        ag_send(slot(a + 1, zz, b, core), *b_both, sibling)
+        ag_send(fs, opposite, *a_both, *b_both, sibling)
+
+    def ag_near(other, side):
+        zz, step = of_plane(other), 3 + 2 * (z + side)
+        own = slot(a + step, zz, b, core)
+        ag_wait(own)
+        if other == side:
+            ag_send(own, at_ab(1 + 2 * zz, 0))
+        ag_send(own, *b_both, sibling)
 
     def ag_opposite():
         own = slot(a, 1 - z, b, core)
         ag_wait(own)
         ag_send(own, *a_both, *b_both, sibling)
 
-    def ag_far(zz):
-        own = slot(a + 2, zz, b, core)
+    def ag_far(other):
+        own = slot(a + 2, of_plane(other), b, core)
         ag_wait(own)
         ag_send(own, *b_both, sibling)
 
-    def ag_b(step):
-        da, zz = arrivals[step]
-        for db in (3, 1):
-            ag_wait(slot(a + da, zz, b + db, core))
-        ag_send(slot(a + da, zz, b + 3 + 2 * zz, core), at_ab(0, 1 + 2 * zz))
-        for db in (3, 1):
-            ag_send(slot(a + da, zz, b + db, core), sibling)
-
-    def ag_b_far(step):
-        da, zz = arrivals[step]
-        own = slot(a + da, zz, b + 2, core)
+    def ag_b(k, side):
+        da, other = arrivals[k]
+        zz = of_plane(other)
+        own = slot(a + da, zz, b + 3 + 2 * (z + side), core)
+        ag_wait(own)
+        if other == side:
+            ag_send(own, at_ab(0, 1 + 2 * zz))
+        ag_send(own, sibling)
+
+    def ag_b_far(k):
+        da, other = arrivals[k]
+        own = slot(a + da, of_plane(other), b + 2, core)
         ag_wait(own)
         ag_send(own, sibling)
 
@@ -383,6 +388,10 @@
             rest = first % 8
             start = SLAB + first - rest
             bacc[rest // 2, start : start + SLAB, :] += grads[j * SLAB : (j + 1) * SLAB]
+
+    def backward_taps(first, last):
+        for t in range(first, last):
+            backward_tap(t)
 
     def backward_rest():
         lane = lax.broadcasted_iota(jnp.int32, (1, 128), 1)
@@ -428,81 +437,92 @@
 
     ag_first()
     norm_forward()
-    ag_near(z)
     make_patches()
-    ag_far(z)
+    ag_near(0, 0)
     ag_opposite()
     sibling_terms(0)
     own_terms(0)
+    own_terms(3)
+    own_terms(2)
+    ag_near(0, 1)
+    rs_far(0)
+    sibling_terms(2)
     sibling_terms(1)
-    rs_far(0)
     rs_near(0)
-    ag_near(1 - z)
-    ag_b(0)
+    ag_far(0)
+    ag_near(1, 1)
+    sibling_terms(3)
+    ag_b(3, 1)
+    ag_b(2, 0)
+    ag_near(1, 0)
+    ag_b(0, 0)
+    own_terms(1)
+    cotangent_shifts()
+    ag_far(1)
+    ag_b(1, 0)
+    ag_b(6, 1)
     rs_far(1)
+    rs_far(2)
+    ag_b(2, 1)
+    ag_b(4, 0)
+    rs_late(0)
+    ag_b(5, 1)
+    ag_b(7, 1)
+    rs_far(3)
+    ag_b(0, 1)
+    ag_b(6, 0)
+    rs_far(5)
+    ag_b(3, 0)
+    ag_b_far(6)
+    ag_b_far(3)
+    rs_far(4)
+    rs_late(1)
+    ag_b(1, 1)
+    rs_near(2)
+    ag_b_far(1)
+    ag_b(4, 1)
+    ag_b_far(2)
+    rs_near(4)
     rs_near(1)
-    rs_late(0)
-    own_terms(1)
-    sibling_terms(2)
-    ag_far(1 - z)
-    ag_b(1)
-    rs_far(2)
-    rs_near(2)
-    rs_late(1)
-    ag_b(2)
-    own_terms(2)
-    sibling_terms(3)
-    rs_far(3)
+    ag_b_far(0)
+    ag_b(5, 0)
+    rs_far(7)
+    ag_b(7, 0)
+    rs_late(2)
+    ag_b_far(5)
+    ag_b_far(4)
+    ag_b_far(7)
+    rs_a_far(0)
+    rs_late(3)
+    ag_sibling()
+    rs_late(4)
+    rs_far(6)
+    backward_taps(0, 3)
+    rs_a_near(0)
     rs_near(3)
-    rs_late(2)
-    rs_a_far(0)
-    ag_b(3)
-    ag_b_far(0)
-    own_terms(3)
-    rs_far(4)
-    rs_near(4)
-    rs_late(3)
-    rs_a_near(0)
-    ag_b(4)
-    ag_b_far(1)
-    cotangent_shifts()
-    rs_far(5)
+    rs_late(5)
     rs_near(5)
-    rs_late(4)
+    backward_taps(3, 6)
+    rs_near(6)
     rs_a_late(0)
-    ag_b(5)
-    ag_b_far(2)
-    rs_far(6)
-    rs_near(6)
-    rs_late(5)
-    ag_b(6)
-    ag_b_far(3)
+    backward_taps(6, 9)
+    rs_a_far(1)
+    rs_late(6)
+    backward_rest()
+    rs_near(7)
+    rs_late(7)
     rs_other_plane()
-    rs_far(7)
-    rs_near(7)
-    rs_late(6)
-    ag_b(7)
-    ag_b_far(4)
-    ag_b_far(5)
-    rs_late(7)
-    rs_a_far(1)
-    ag_b_far(6)
-    ag_b_far(7)
+    norm_start(0, ncol[...].T[:8])
+    rs_a_late(1)
     rs_a_near(1)
-    ag_sibling()
-    for t in range(5):
-        backward_tap(t)
-    rs_a_late(1)
-    for t in range(5, 9):
-        backward_tap(t)
+    forward(0, 2)
+    norm_start(1, norm_sum(0))
     rs_own_plane()
-    backward_rest()
-    norm_start(0, ncol[...].T[:8])
+    norm_partner_start()
+    forward(2, 4)
+    forward(4, 6)
     write_input_grad()
-    norm_start(1, norm_sum(0))
-    forward(0, 4)
-    norm_partner_start()
-    forward(4, 8)
+    forward(6, 8)
     rs_partner()
     norm_last()
 
@@ -523,6 +543,11 @@
     for stage in range(2):
         for d in range(1, 8):
             norm_copy(stage, d, True).wait_send()
+
+
+def finish(*refs):
+    for source, target in zip(refs[: len(refs) // 2], refs[len(refs) // 2 :]):
+        target[...] = source[...]
 
 
 def shards(latents, cotangent, conv_weight, norm_gain, norm_shift, partner_bit):
@@ -583,7 +608,13 @@
         latents.reshape(POS, chans), cotangent.reshape(POS, chans), conv_weight[0],
         norm_gain, norm_shift, partner_bit,
     )
-    block_out, input_grad, weight_grad, norm_grad = results
+    block_out, input_grad, weight_grad, norm_grad = pl.pallas_call(
+        finish,
+        out_shape=[jax.ShapeDtypeStruct(result.shape, result.dtype) for result in results],
+        in_specs=[vmem] * 4,
+        out_specs=[vmem] * 4,
+        name="finish",
+    )(*results)
     return (
         block_out.reshape(latents.shape),
         input_grad.reshape(latents.shape),

time: 91.8 us -> 79.7 us (0.87)
  Pallas kernels: 86.8 us -> 78.9 us
  local copies, waits for them, and re-layouts: 4.12 us -> 0 us
    pallas_call x1, Pallas kernels: 86.8 us -> 76.8 us  [shards(): pl.pallas_call(kernel, out_shape=(jax.ShapeDtypeStruct((POS, chans), BF),...]
    unnamed x10 -> x0, local copies, waits for them, and re-layouts: 4.12 us -> none
    pallas_call x0 -> x1, Pallas kernels: none -> 2.07 us  [shards(): pl.pallas_call(finish, out_shape=[jax.ShapeDtypeStruct(result.shape, resu...]
where the time goes in v2:
time: 79.7 us; the launch traced here: 79.6 us
  Pallas kernels  78.9 us (99%)
    pallas_call x1, Pallas kernels, shards(): pl.pallas_call(kernel, out_shape=(jax.ShapeDtypeStruct((POS, chans), BF),...  76.8 us
    pallas_call x1, Pallas kernels, shards(): pl.pallas_call(finish, out_shape=[jax.ShapeDtypeStruct(result.shape, resu...  2.07 us

profile of v2, /device:TPU:24, one launch (start us, length us, event | category | flops | bytes accessed | tf_op | source)
XLA Modules:
  0.0 79.6 jit_solution(4437860871592398987)
XLA Ops:
  0.6 76.8 %block.1 = (bf16[256,640]{1,0:T(8,128)(2,1)}, bf16[256,640]{1,0:T(8,128)(2,1)}, f32[90,1,640]{2,1,0:T(1,128)}, f32[2,640]{1,0:T(2,128)}) custom-call(bf16[256,640]{1,0:T(8,128)(2,1)} %bitcast.7, bf16[256,640]{1,0:T(8,128)(2,1)} %bitcast.8, bf16[90,640]{1,0:T(8,128)(2,1)} %bitcast.9, f32[1,640]{1,0:T(1,128)} %gain.1, f32[1,640]{1,0:T(1,128)} %shift.1, s32[64]{0:T(128)} %bits.1), custom_call_target="tpu_custom_call" | custom-call | tf_op jit(solution)/shard_map/block/pallas_call | solution.py:560
  77.5 2.1 %finish.1 = (bf16[256,640]{1,0:T(8,128)(2,1)}, bf16[256,640]{1,0:T(8,128)(2,1)}, f32[90,1,640]{2,1,0:T(1,128)}, f32[2,640]{1,0:T(2,128)}) custom-call(bf16[256,640]{1,0:T(8,128)(2,1)} %get-tuple-element.12.refs_0_, bf16[256,640]{1,0:T(8,128)(2,1)} %get-tuple-element.13.refs_1_, f32[90,1,640]{2,1,0:T(1,128)} %get-tuple-element.14.refs_2_, ...), custom_call_target="tpu_custom_call" | custom-call | tf_op jit(solution)/shard_map/finish/pallas_call | solution.py:611

commit v3 on v2

--- a/solution.py
+++ b/solution.py
@@ -26,12 +26,12 @@
 
 
 def kernel(
-    lat, cot, w_in, gain, shift, bits, out, in_grad, w_grad, n_grad,
-    wg, pt, tall, cs, tm, bacc, xt, nt, at, acc, gcol, scol, rcol, ncol, fin,
+    lat_in, cot_in, w_in, gain, shift, bits, out, in_grad, w_grad, n_grad,
+    lat, cot, w_own, wg, pt, tall, cs, tm, bacc, xt, nt, at, acc, gcol, scol, rcol, ncol, fin,
     sib_s, sib_r, b2_s, b2_r, b1_s, b1_r, a2_s, a2_r, a1_s, a1_r, z_s, z_r, p_s, p_r,
     n1_s, n1_r, n2_s, n2_r, n3_s, n3_r,
     ag_ss, ag_rs, sib_ss, sib_rs, b2_ss, b2_rs, b1_ss, b1_rs, a2_ss, a2_rs, a1_ss, a1_rs,
-    z_ss, z_rs, p_ss, p_rs, n1_ss, n1_rs, n2_ss, n2_rs, n3_ss, n3_rs,
+    z_ss, z_rs, p_ss, p_rs, n1_ss, n1_rs, n2_ss, n2_rs, n3_ss, n3_rs, in_s,
 ):
     chans = lat.shape[1]
     shard = w_in.shape[0]
@@ -389,11 +389,7 @@
             start = SLAB + first - rest
             bacc[rest // 2, start : start + SLAB, :] += grads[j * SLAB : (j + 1) * SLAB]
 
-    def backward_taps(first, last):
-        for t in range(first, last):
-            backward_tap(t)
-
-    def backward_rest():
+    def backward_rest(part):
         lane = lax.broadcasted_iota(jnp.int32, (1, 128), 1)
 
         def one(i):
@@ -419,7 +415,8 @@
                 one(i * UNROLL + u)
             return carry
 
-        lax.fori_loop(0, blocks // UNROLL, body, 0)
+        steps = blocks // UNROLL // 2
+        lax.fori_loop(part * steps, (part + 1) * steps, body, 0)
 
     def write_input_grad():
         for i in range(chans // 128):
@@ -430,99 +427,115 @@
     neighbours = [peer(d)[1] for peer in (peer1, peer2) for d in range(1, 8)] + list(partners)
     for device in neighbours:
         pl.semaphore_signal(barrier, inc=1, device_id=device, device_id_type=pl.DeviceIdType.MESH)
+    arriving = [
+        pltpu.make_async_copy(source, target, in_s.at[i])
+        for i, (source, target) in enumerate(((w_in, w_own), (lat_in, lat), (cot_in, cot)))
+    ]
+    for copy in arriving:
+        copy.start()
     wg[fs, SLAB - 16 :, :] = jnp.zeros((16, chans), BF)
-    wg[fs, :shard, :] = w_in[...]
+    arriving[0].wait()
+    wg[fs, :shard, :] = w_own[...]
+    pl.semaphore_wait(barrier, len(neighbours))
+
+    ag_first()
+    arriving[1].wait()
     transposes()
-    pl.semaphore_wait(barrier, len(neighbours))
-
-    ag_first()
+    arriving[2].wait()
     norm_forward()
     make_patches()
     ag_near(0, 0)
-    ag_opposite()
     sibling_terms(0)
     own_terms(0)
+    ag_opposite()
+    sibling_terms(1)
+    rs_far(1)
+    rs_far(0)
+    ag_near(0, 1)
+    ag_far(0)
+    own_terms(1)
+    rs_far(2)
+    sibling_terms(2)
+    ag_near(1, 1)
+    ag_b(0, 0)
+    ag_near(1, 0)
+    ag_b(0, 1)
+    ag_b(3, 1)
+    rs_near(0)
+    ag_b(1, 0)
+    ag_b(1, 1)
+    own_terms(2)
+    rs_late(0)
+    ag_b(2, 0)
+    cotangent_shifts()
+    rs_far(4)
+    ag_b(4, 0)
+    ag_far(1)
+    ag_b(3, 0)
+    ag_b(6, 1)
+    ag_b(5, 1)
+    ag_b(2, 1)
+    ag_b_far(0)
+    rs_far(3)
+    ag_b(7, 1)
+    sibling_terms(3)
+    rs_near(1)
+    rs_late(1)
+    ag_b(5, 0)
+    ag_b_far(6)
     own_terms(3)
-    own_terms(2)
-    ag_near(0, 1)
-    rs_far(0)
-    sibling_terms(2)
-    sibling_terms(1)
-    rs_near(0)
-    ag_far(0)
-    ag_near(1, 1)
-    sibling_terms(3)
-    ag_b(3, 1)
-    ag_b(2, 0)
-    ag_near(1, 0)
-    ag_b(0, 0)
-    own_terms(1)
-    cotangent_shifts()
-    ag_far(1)
-    ag_b(1, 0)
-    ag_b(6, 1)
-    rs_far(1)
-    rs_far(2)
-    ag_b(2, 1)
-    ag_b(4, 0)
-    rs_late(0)
-    ag_b(5, 1)
-    ag_b(7, 1)
-    rs_far(3)
-    ag_b(0, 1)
+    rs_near(2)
+    rs_late(2)
     ag_b(6, 0)
+    ag_b_far(5)
+    ag_b_far(3)
+    ag_b_far(2)
+    ag_b_far(1)
     rs_far(5)
-    ag_b(3, 0)
-    ag_b_far(6)
-    ag_b_far(3)
-    rs_far(4)
-    rs_late(1)
-    ag_b(1, 1)
-    rs_near(2)
-    ag_b_far(1)
-    ag_b(4, 1)
-    ag_b_far(2)
+    rs_a_far(0)
+    rs_late(4)
     rs_near(4)
-    rs_near(1)
-    ag_b_far(0)
-    ag_b(5, 0)
     rs_far(7)
-    ag_b(7, 0)
-    rs_late(2)
-    ag_b_far(5)
+    rs_far(6)
+    rs_near(3)
     ag_b_far(4)
     ag_b_far(7)
-    rs_a_far(0)
     rs_late(3)
+    rs_near(5)
+    rs_near(6)
+    ag_b(7, 0)
+    ag_b(4, 1)
     ag_sibling()
-    rs_late(4)
-    rs_far(6)
-    backward_taps(0, 3)
+    backward_tap(5)
     rs_a_near(0)
-    rs_near(3)
+    backward_tap(0)
+    backward_tap(7)
+    backward_tap(2)
+    backward_tap(3)
+    backward_tap(1)
+    rs_a_late(0)
+    backward_tap(6)
+    backward_tap(4)
+    backward_tap(8)
     rs_late(5)
-    rs_near(5)
-    backward_taps(3, 6)
-    rs_near(6)
-    rs_a_late(0)
-    backward_taps(6, 9)
+    backward_rest(1)
     rs_a_far(1)
     rs_late(6)
-    backward_rest()
+    backward_rest(0)
+    norm_start(0, ncol[...].T[:8])
+    rs_other_plane()
     rs_near(7)
     rs_late(7)
-    rs_other_plane()
-    norm_start(0, ncol[...].T[:8])
+    rs_a_near(1)
     rs_a_late(1)
-    rs_a_near(1)
     forward(0, 2)
     norm_start(1, norm_sum(0))
+    forward(2, 4)
+    write_input_grad()
     rs_own_plane()
+    forward(4, 6)
+    forward(6, 8)
     norm_partner_start()
-    forward(2, 4)
-    forward(4, 6)
-    write_input_grad()
-    forward(6, 8)
     rs_partner()
     norm_last()
 
@@ -555,6 +568,7 @@
     shard = conv_weight.shape[1]
     count = lax.axis_size("fsdp")
     vmem = pl.BlockSpec(memory_space=pltpu.VMEM)
+    anywhere = pl.BlockSpec(memory_space=pl.ANY)
     piece = (SLAB, chans)
     dma = pltpu.SemaphoreType.DMA
     results = pl.pallas_call(
@@ -565,9 +579,12 @@
             jax.ShapeDtypeStruct((shard, 1, chans), F32),
             jax.ShapeDtypeStruct((2, chans), F32),
         ),
-        in_specs=[vmem] * 5 + [pl.BlockSpec(memory_space=pltpu.SMEM)],
+        in_specs=[anywhere] * 3 + [vmem] * 2 + [pl.BlockSpec(memory_space=pltpu.SMEM)],
         out_specs=(vmem,) * 4,
         scratch_shapes=[
+            pltpu.VMEM((POS, chans), BF),
+            pltpu.VMEM((POS, chans), BF),
+            pltpu.VMEM((shard, chans), BF),
             pltpu.VMEM((count, *piece), BF),
             pltpu.VMEM((count, SLAB, POS), BF),
             pltpu.VMEM((count * shard + 8, POS), F32),
@@ -598,7 +615,7 @@
             dma, dma,
             dma((2,)), dma((2,)),
             dma((8,)), dma((8,)), dma((8,)), dma((8,)),
-            dma((2,)), dma((2,)),
+            dma((2,)), dma((2,)), dma((3,)),
         ],
         compiler_params=pltpu.CompilerParams(
             collective_id=0, has_side_effects=True, vmem_limit_bytes=60 << 20

time: 79.7 us -> 77.5 us (0.972)
  the two profiles are of different devices: /device:TPU:24 before, /device:TPU:15 now
where the time goes in v3:
time: 77.5 us; the launch traced here: 77.3 us
  Pallas kernels  76.7 us (99%)
    pallas_call x1, Pallas kernels, shards(): pl.pallas_call(kernel, out_shape=(jax.ShapeDtypeStruct((POS, chans), BF),...  74.6 us
    pallas_call x1, Pallas kernels, shards(): pl.pallas_call(finish, out_shape=[jax.ShapeDtypeStruct(result.shape, resu...  2.07 us

profile of v3, /device:TPU:15, one launch (start us, length us, event | category | flops | bytes accessed | tf_op | source)
XLA Modules:
  0.0 77.3 jit_solution(5874256858670361833)
XLA Ops:
  0.6 74.6 %block.1 = (bf16[256,640]{1,0:T(8,128)(2,1)}, bf16[256,640]{1,0:T(8,128)(2,1)}, f32[90,1,640]{2,1,0:T(1,128)}, f32[2,640]{1,0:T(2,128)}) custom-call(bf16[256,640]{1,0:T(8,128)(2,1)} %bitcast.7, bf16[256,640]{1,0:T(8,128)(2,1)} %bitcast.8, bf16[90,640]{1,0:T(8,128)(2,1)} %bitcast.9, f32[1,640]{1,0:T(1,128)} %gain.1, f32[1,640]{1,0:T(1,128)} %shift.1, s32[64]{0:T(128)} %bits.1), custom_call_target="tpu_custom_call" | custom-call | tf_op jit(solution)/shard_map/block/pallas_call | solution.py:574
  75.3 2.1 %finish.1 = (bf16[256,640]{1,0:T(8,128)(2,1)}, bf16[256,640]{1,0:T(8,128)(2,1)}, f32[90,1,640]{2,1,0:T(1,128)}, f32[2,640]{1,0:T(2,128)}) custom-call(bf16[256,640]{1,0:T(8,128)(2,1)} %get-tuple-element.12.refs_0_, bf16[256,640]{1,0:T(8,128)(2,1)} %get-tuple-element.13.refs_1_, f32[90,1,640]{2,1,0:T(1,128)} %get-tuple-element.14.refs_2_, ...), custom_call_target="tpu_custom_call" | custom-call | tf_op jit(solution)/shard_map/finish/pallas_call | solution.py:628

commit v4 on v3

--- a/solution.py
+++ b/solution.py
@@ -445,99 +445,97 @@
     norm_forward()
     make_patches()
     ag_near(0, 0)
+    ag_opposite()
     sibling_terms(0)
     own_terms(0)
-    ag_opposite()
+    own_terms(2)
+    ag_near(0, 1)
+    own_terms(1)
+    rs_far(0)
+    rs_near(0)
+    cotangent_shifts()
+    ag_far(0)
+    ag_near(1, 1)
     sibling_terms(1)
+    own_terms(3)
+    ag_b(2, 1)
+    ag_near(1, 0)
+    rs_far(2)
     rs_far(1)
-    rs_far(0)
-    ag_near(0, 1)
-    ag_far(0)
-    own_terms(1)
-    rs_far(2)
     sibling_terms(2)
-    ag_near(1, 1)
-    ag_b(0, 0)
-    ag_near(1, 0)
-    ag_b(0, 1)
-    ag_b(3, 1)
-    rs_near(0)
     ag_b(1, 0)
-    ag_b(1, 1)
-    own_terms(2)
     rs_late(0)
     ag_b(2, 0)
-    cotangent_shifts()
+    ag_b(0, 0)
+    ag_b(3, 1)
     rs_far(4)
     ag_b(4, 0)
     ag_far(1)
-    ag_b(3, 0)
     ag_b(6, 1)
     ag_b(5, 1)
-    ag_b(2, 1)
-    ag_b_far(0)
     rs_far(3)
+    ag_b(4, 1)
     ag_b(7, 1)
+    rs_near(2)
+    ag_b(3, 0)
+    ag_b_far(1)
+    rs_late(2)
+    ag_b(1, 1)
     sibling_terms(3)
+    rs_late(1)
     rs_near(1)
-    rs_late(1)
-    ag_b(5, 0)
-    ag_b_far(6)
-    own_terms(3)
-    rs_near(2)
-    rs_late(2)
+    ag_b_far(3)
+    ag_b_far(2)
+    rs_far(5)
+    rs_near(4)
+    rs_a_far(0)
+    ag_b(0, 1)
     ag_b(6, 0)
     ag_b_far(5)
-    ag_b_far(3)
-    ag_b_far(2)
-    ag_b_far(1)
-    rs_far(5)
-    rs_a_far(0)
     rs_late(4)
-    rs_near(4)
+    ag_b_far(6)
+    ag_b_far(0)
+    ag_b(5, 0)
     rs_far(7)
     rs_far(6)
     rs_near(3)
     ag_b_far(4)
+    rs_late(3)
     ag_b_far(7)
-    rs_late(3)
     rs_near(5)
     rs_near(6)
     ag_b(7, 0)
-    ag_b(4, 1)
     ag_sibling()
+    backward_tap(2)
+    backward_tap(0)
+    backward_tap(6)
+    backward_tap(7)
+    backward_tap(3)
+    rs_a_late(0)
+    backward_tap(1)
+    rs_a_near(0)
     backward_tap(5)
-    rs_a_near(0)
-    backward_tap(0)
-    backward_tap(7)
-    backward_tap(2)
-    backward_tap(3)
-    backward_tap(1)
-    rs_a_late(0)
-    backward_tap(6)
+    backward_tap(8)
     backward_tap(4)
-    backward_tap(8)
     rs_late(5)
-    backward_rest(1)
+    backward_rest(0)
     rs_a_far(1)
     rs_late(6)
-    backward_rest(0)
+    backward_rest(1)
     norm_start(0, ncol[...].T[:8])
     rs_other_plane()
     rs_near(7)
     rs_late(7)
     rs_a_near(1)
     rs_a_late(1)
+    norm_start(1, norm_sum(0))
+    rs_own_plane()
     forward(0, 2)
-    norm_start(1, norm_sum(0))
+    norm_partner_start()
     forward(2, 4)
     write_input_grad()
-    rs_own_plane()
     forward(4, 6)
     forward(6, 8)
-    norm_partner_start()
-    rs_partner()
-    norm_last()
 
     for copy in sent:
         copy.wait_send()
@@ -550,6 +548,10 @@
         a2_copy(h).wait_send()
         for way in range(2):
             a1_copy(h, way).wait_send()
+
+    rs_partner()
+    norm_last()
+
     z_copy.wait_send()
     for copy in p_copies + n3_copies:
         copy.wait_send()

time: 77.5 us -> 76.5 us (0.987)
  the two profiles are of different devices: /device:TPU:15 before, /device:TPU:24 now
where the time goes in v4:
time: 76.5 us; the launch traced here: 75.4 us
  Pallas kernels  74.8 us (98%)
    pallas_call x1, Pallas kernels, shards(): pl.pallas_call(kernel, out_shape=(jax.ShapeDtypeStruct((POS, chans), BF),...  72.7 us
    pallas_call x1, Pallas kernels, shards(): pl.pallas_call(finish, out_shape=[jax.ShapeDtypeStruct(result.shape, resu...  2.07 us

profile of v4, /device:TPU:24, one launch (start us, length us, event | category | flops | bytes accessed | tf_op | source)
XLA Modules:
  0.0 75.4 jit_solution(6388751104692076960)
XLA Ops:
  0.6 72.7 %block.1 = (bf16[256,640]{1,0:T(8,128)(2,1)}, bf16[256,640]{1,0:T(8,128)(2,1)}, f32[90,1,640]{2,1,0:T(1,128)}, f32[2,640]{1,0:T(2,128)}) custom-call(bf16[256,640]{1,0:T(8,128)(2,1)} %bitcast.7, bf16[256,640]{1,0:T(8,128)(2,1)} %bitcast.8, bf16[90,640]{1,0:T(8,128)(2,1)} %bitcast.9, f32[1,640]{1,0:T(1,128)} %gain.1, f32[1,640]{1,0:T(1,128)} %shift.1, s32[64]{0:T(128)} %bits.1), custom_call_target="tpu_custom_call" | custom-call | tf_op jit(solution)/shard_map/block/pallas_call | solution.py:576
  73.4 2.1 %finish.1 = (bf16[256,640]{1,0:T(8,128)(2,1)}, bf16[256,640]{1,0:T(8,128)(2,1)}, f32[90,1,640]{2,1,0:T(1,128)}, f32[2,640]{1,0:T(2,128)}) custom-call(bf16[256,640]{1,0:T(8,128)(2,1)} %get-tuple-element.12.refs_0_, bf16[256,640]{1,0:T(8,128)(2,1)} %get-tuple-element.13.refs_1_, f32[90,1,640]{2,1,0:T(1,128)} %get-tuple-element.14.refs_2_, ...), custom_call_target="tpu_custom_call" | custom-call | tf_op jit(solution)/shard_map/finish/pallas_call | solution.py:630

commit v5 on v4

--- a/solution.py
+++ b/solution.py
@@ -445,83 +445,83 @@
     norm_forward()
     make_patches()
     ag_near(0, 0)
+    own_terms(1)
     ag_opposite()
     sibling_terms(0)
+    ag_near(0, 1)
     own_terms(0)
     own_terms(2)
-    ag_near(0, 1)
-    own_terms(1)
     rs_far(0)
+    sibling_terms(1)
     rs_near(0)
-    cotangent_shifts()
     ag_far(0)
+    rs_far(2)
+    sibling_terms(2)
+    rs_far(1)
+    sibling_terms(3)
     ag_near(1, 1)
-    sibling_terms(1)
-    own_terms(3)
+    ag_near(1, 0)
+    rs_late(0)
+    rs_far(4)
+    ag_b(2, 0)
     ag_b(2, 1)
-    ag_near(1, 0)
-    rs_far(2)
-    rs_far(1)
-    sibling_terms(2)
+    ag_b(3, 1)
+    ag_b(0, 1)
+    ag_b(0, 0)
     ag_b(1, 0)
-    rs_late(0)
-    ag_b(2, 0)
-    ag_b(0, 0)
-    ag_b(3, 1)
-    rs_far(4)
     ag_b(4, 0)
     ag_far(1)
     ag_b(6, 1)
+    ag_b(5, 0)
+    rs_far(3)
+    rs_late(2)
+    own_terms(3)
+    ag_b(4, 1)
     ag_b(5, 1)
-    rs_far(3)
-    ag_b(4, 1)
+    ag_b(3, 0)
+    cotangent_shifts()
+    ag_b(1, 1)
     ag_b(7, 1)
     rs_near(2)
-    ag_b(3, 0)
-    ag_b_far(1)
-    rs_late(2)
-    ag_b(1, 1)
-    sibling_terms(3)
+    ag_b_far(2)
     rs_late(1)
+    rs_far(5)
+    ag_b_far(0)
+    rs_a_far(0)
     rs_near(1)
-    ag_b_far(3)
-    ag_b_far(2)
-    rs_far(5)
-    rs_near(4)
-    rs_a_far(0)
-    ag_b(0, 1)
-    ag_b(6, 0)
-    ag_b_far(5)
     rs_late(4)
-    ag_b_far(6)
-    ag_b_far(0)
-    ag_b(5, 0)
     rs_far(7)
     rs_far(6)
+    ag_b(6, 0)
+    ag_b_far(3)
+    rs_near(4)
+    ag_b_far(6)
+    ag_b_far(5)
+    rs_late(3)
+    ag_b_far(1)
+    ag_b_far(4)
     rs_near(3)
-    ag_b_far(4)
-    rs_late(3)
     ag_b_far(7)
     rs_near(5)
     rs_near(6)
     ag_b(7, 0)
     ag_sibling()
+    backward_tap(6)
+    backward_tap(0)
+    backward_tap(4)
+    backward_tap(3)
     backward_tap(2)
-    backward_tap(0)
-    backward_tap(6)
-    backward_tap(7)
-    backward_tap(3)
     rs_a_late(0)
     backward_tap(1)
     rs_a_near(0)
+    backward_tap(8)
     backward_tap(5)
-    backward_tap(8)
-    backward_tap(4)
+    backward_tap(7)
     rs_late(5)
-    backward_rest(0)
+    backward_rest(1)
     rs_a_far(1)
     rs_late(6)
-    backward_rest(1)
+    backward_rest(0)
     norm_start(0, ncol[...].T[:8])
     rs_other_plane()
     rs_near(7)
@@ -530,10 +530,10 @@
     rs_a_late(1)
     norm_start(1, norm_sum(0))
     rs_own_plane()
+    norm_partner_start()
+    write_input_grad()
     forward(0, 2)
-    norm_partner_start()
     forward(2, 4)
-    write_input_grad()
     forward(4, 6)
     forward(6, 8)
 

time: 76.5 us -> 79.6 us (1.041)
  the two profiles are of different devices: /device:TPU:24 before, /device:TPU:62 now
where the time goes in v5:
time: 79.6 us; the launch traced here: 79.4 us
  Pallas kernels  78.8 us (99%)
    pallas_call x1, Pallas kernels, shards(): pl.pallas_call(kernel, out_shape=(jax.ShapeDtypeStruct((POS, chans), BF),...  76.7 us
    pallas_call x1, Pallas kernels, shards(): pl.pallas_call(finish, out_shape=[jax.ShapeDtypeStruct(result.shape, resu...  2.07 us

profile of v5, /device:TPU:62, one launch (start us, length us, event | category | flops | bytes accessed | tf_op | source)
XLA Modules:
  0.0 79.4 jit_solution(6377696183552141685)
XLA Ops:
  0.6 76.7 %block.1 = (bf16[256,640]{1,0:T(8,128)(2,1)}, bf16[256,640]{1,0:T(8,128)(2,1)}, f32[90,1,640]{2,1,0:T(1,128)}, f32[2,640]{1,0:T(2,128)}) custom-call(bf16[256,640]{1,0:T(8,128)(2,1)} %bitcast.7, bf16[256,640]{1,0:T(8,128)(2,1)} %bitcast.8, bf16[90,640]{1,0:T(8,128)(2,1)} %bitcast.9, f32[1,640]{1,0:T(1,128)} %gain.1, f32[1,640]{1,0:T(1,128)} %shift.1, s32[64]{0:T(128)} %bits.1), custom_call_target="tpu_custom_call" | custom-call | tf_op jit(solution)/shard_map/block/pallas_call | solution.py:576
  77.3 2.1 %finish.1 = (bf16[256,640]{1,0:T(8,128)(2,1)}, bf16[256,640]{1,0:T(8,128)(2,1)}, f32[90,1,640]{2,1,0:T(1,128)}, f32[2,640]{1,0:T(2,128)}) custom-call(bf16[256,640]{1,0:T(8,128)(2,1)} %get-tuple-element.12.refs_0_, bf16[256,640]{1,0:T(8,128)(2,1)} %get-tuple-element.13.refs_1_, f32[90,1,640]{2,1,0:T(1,128)} %get-tuple-element.14.refs_2_, ...), custom_call_target="tpu_custom_call" | custom-call | tf_op jit(solution)/shard_map/finish/pallas_call | solution.py:630
